TPU v7x, 512 devices: a whole 4x4x16 slice. The times are simulated.
512 devices in a mesh: wide: 64 (over y_lo, z, core), narrow: 8 (over y_hi, x).
Axes of the slice: x: 4, y: 4 (y_hi: 2, y_lo: 2; y = y_hi * 2 + y_lo), z: 16, core: 2. Of those that a mesh axis runs over, the one named last changes fastest.
Arguments:
- tokens: bfloat16 [8192, 2048], P('wide', 'narrow'), may hold values from -6 to 6
- expert_ids: int32 [8192, 6], P('wide'), may hold values from 0 to 63, all different within a row; in each aligned block of 128 rows (0 to 127, 128 to 255, ...) at most 14 rows name the same one
- route_weights: bfloat16 [8192, 6], P('wide'), may hold values from 0.049804688 to 0.5
- w_gate: bfloat16 [64, 1408, 2048], P('wide', 'narrow'), may hold values from -0.125 to 0.125
- w_up: bfloat16 [64, 1408, 2048], P('wide', 'narrow'), may hold values from -0.125 to 0.125
- w_down: bfloat16 [64, 1408, 2048], P('wide', 'narrow'), may hold values from -0.15625 to 0.15625
Outputs:
- mixed: bfloat16 [8192, 2048], P('wide', 'narrow')
Inputs may be any that keep to these rules, and one draw needn't show every extreme that they name: `expert_ids`: within a row the 6 experts differ. Among the 128 tokens of one aligned block, no expert is named more than 14 times, a bound that some block reaches.
All inputs are finite; a program needn't handle non-finite values.
Results may differ from a plain program's by a relative error of at most 0.017.
Values may be sent and summed in bfloat16 or wider, within the bound.
A program may use at most 64 MiB of HBM per device.

v0:
```python
import jax
import jax.numpy as jnp
from jax import lax
from jax.sharding import PartitionSpec as P


def local(tokens, expert_ids, route_weights, w_gate, w_up, w_down):
    tok_rows = expert_ids.shape[0]
    top_count = expert_ids.shape[1]
    local_experts = w_gate.shape[0]
    groups_wide = lax.axis_size("wide")
    experts_all = local_experts * groups_wide
    capacity = 7 * tok_rows * top_count // (6 * experts_all)
    slots_all = experts_all * capacity
    width = w_down.shape[2]
    flat_ids = expert_ids.reshape(-1)
    onehot = (flat_ids[:, None] == jnp.arange(experts_all, dtype=jnp.int32)[None, :]).astype(
        jnp.int32
    )
    running = jnp.cumsum(onehot, axis=0)
    slot_index = jnp.sum(running * onehot, axis=1) - 1
    destination = (flat_ids * capacity + slot_index).reshape(tok_rows, top_count)
    slot_table = (
        destination[:, :, None] == jnp.arange(slots_all, dtype=jnp.int32)[None, None, :]
    ).astype(jnp.float32)
    dispatch = jnp.sum(slot_table, axis=1).astype(jnp.bfloat16)
    whole = lax.all_gather(tokens, "narrow", axis=1, tiled=True)
    outgoing = jnp.einsum("ts,td->sd", dispatch, whole, preferred_element_type=jnp.float32).astype(
        jnp.bfloat16
    )
    received = lax.all_to_all(outgoing, "wide", split_axis=0, concat_axis=0, tiled=True)
    slot_rows = received.reshape(groups_wide, local_experts, capacity, width)
    gate_proj = jnp.einsum("secd,efd->secf", slot_rows, w_gate, preferred_element_type=jnp.float32)
    up_proj = jnp.einsum("secd,efd->secf", slot_rows, w_up, preferred_element_type=jnp.float32)
    hidden = (jax.nn.silu(gate_proj) * up_proj).astype(jnp.bfloat16)
    partial_value = jnp.einsum(
        "secf,efd->secd", hidden, w_down, preferred_element_type=jnp.float32
    ).astype(jnp.bfloat16)
    partial_value = partial_value.reshape(slots_all, width)
    summed = lax.psum_scatter(partial_value, "narrow", scatter_dimension=1, tiled=True).astype(
        jnp.float32
    )
    returned = lax.all_to_all(
        summed.astype(jnp.bfloat16), "wide", split_axis=0, concat_axis=0, tiled=True
    ).astype(summed.dtype)
    picked = returned[destination.reshape(-1)].reshape(tok_rows, top_count, -1)
    mixed = jnp.sum(route_weights.astype(jnp.float32)[:, :, None] * picked, axis=1)
    return mixed.astype(jnp.bfloat16)


def solution(mesh):
    in_specs = (
        P("wide", "narrow"),
        P("wide", None),
        P("wide", None),
        P("wide", "narrow", None),
        P("wide", "narrow", None),
        P("wide", "narrow", None),
    )
    out_specs = P("wide", "narrow")
    return jax.shard_map(local, mesh=mesh, in_specs=in_specs, out_specs=out_specs, check_vma=False)
```

profile of v0, /device:TPU:1, one launch (start us, length us, event | category | flops | bytes accessed | tf_op | source)
XLA Modules:
  0.0 438.2 jit_solution(4259593260769932684)
XLA Ops:
  6.5 0.0 copy-start
  6.5 0.0 reduce-scatter.2.cloned.1.call-start
  6.5 0.9 copy.26
  7.4 0.1 eq.42
  7.5 0.1 eq.38
  7.7 1.8 reduce-window.6
  9.5 0.3 slice_reduce_fusion
  9.8 0.1 fusion.28
  10.0 0.1 sub.9
  10.1 0.1 copy.30
  10.2 0.4 convert_reduce_fusion
  10.6 31.0 %all_gather.3 = bf16[128,2048]{1,0:T(8,128)(2,1)S(1)} all-gather(bf16[128,256]{1,0:T(8,128)(2,1)} %param.6), channel_id=1, replica_groups=mesh['wide'=64,'narrow'=8] {'narrow'}, dimensions={1}, use_global_device_ids=true | all-gather | bytes 589824 | tf_op jit(solution)/shard_map/all_gather | solution.py:27
  41.6 3.0 convolution_convert_fusion
  44.6 6.0 %all_to_all.12 = bf16[64,14,2048]{2,1,0:T(8,128)(2,1)} reshape(bf16[896,2048]{1,0:T(8,128)(2,1)} %convolution_convert_fusion) | data formatting | bytes 7340032 | tf_op jit(solution)/shard_map/all_to_all | solution.py:31
  50.6 0.0 copy-start.3
  50.6 207.4 %all_to_all.18 = bf16[64,14,2048]{2,1,0:T(8,128)(2,1)S(1)} all-to-all(bf16[64,14,2048]{2,1,0:T(8,128)(2,1)} %all_to_all.12), channel_id=1, replica_groups=mesh['wide'=64,'narrow'=8] {'wide'}, dimensions={0} | all-to-all | bytes 7340032 | tf_op jit(solution)/shard_map/all_to_all | solution.py:31
  258.0 0.0 copy-start.1
  258.0 1.9 copy-done.1
  259.9 0.0 copy-done.3
  259.9 0.0 copy-start.4
  259.9 5.1 %fusion.4 = f32[64,1,14,176]{3,0,2,1:T(8,128)} fusion(bf16[64,14,2048]{2,1,0:T(8,128)(2,1)S(1)} %all_to_all.18, bf16[1,176,2048]{2,1,0:T(8,128)(2,1)S(1)} %copy-done.3), kind=kOutput, calls=%fused_computation.9 | convolution fusion | flops 645922816 | bytes 5021696 | tf_op jit(solution)/shard_map/secd,efd->secf/dot_general | solution.py:33
  265.0 0.0 copy-done
  265.0 0.0 copy-done.4
  265.0 8.3 %convert_bitcast_fusion = bf16[64,1,14,2048]{3,0,2,1:T(8,128)(2,1)} fusion(bf16[64,14,2048]{2,1,0:T(8,128)(2,1)} %copy-done.1, f32[64,1,14,176]{3,0,2,1:T(8,128)} %fusion.4, bf16[1,176,2048]{2,1,0:T(8,128)(2,1)S(1)} %copy-done, bf16[1,176,2048]{2,1,0:T(8,128)(2,1)S(1)} %copy-done.4), kind=kOutput, calls=%fused_computation.1 | convolution fusion | flops 1294626816 | bytes 9412608 | tf_op jit(solution)/shard_map/secf,efd->secd/dot_general | solution.py:36
  273.2 6.0 %copy.33 = bf16[64,1,14,2048]{3,2,0,1:T(8,128)(2,1)} copy(bf16[64,1,14,2048]{3,0,2,1:T(8,128)(2,1)} %convert_bitcast_fusion) | data formatting | bytes 7340032 | tf_op jit(solution)/shard_map/convert_element_type | solution.py:38
  279.2 6.0 %reshape.100 = bf16[896,2048]{1,0:T(8,128)(2,1)} reshape(bf16[64,1,14,2048]{3,2,0,1:T(8,128)(2,1)} %copy.33) | data formatting | bytes 7340032 | tf_op jit(solution)/shard_map/reshape | solution.py:39
  285.2 0.0 copy-start.2
  285.2 0.0 reduce-scatter.2.cloned.1.call-update
  285.2 94.2 %reduce-scatter.2.cloned.1.call-done = bf16[896,256]{1,0:T(8,128)(2,1)} async-done(((bf16[896,2048]{1,0:T(8,128)(2,1)}), bf16[896,256]{1,0:T(8,128)(2,1)}) %reduce-scatter.2.cloned.1.call-update) | async-done | bytes 458768 | tf_op jit(solution)/shard_map/reduce_scatter | solution.py:40
  379.5 1.9 all_to_all.14
  381.4 14.9 %all-to-all-start.1 = ((bf16[64,14,256]{2,1,0:T(8,128)(2,1)}), bf16[64,14,256]{2,1,0:T(8,128)(2,1)S(1)}, u32[]{:S(2)}, u32[]{:S(2)}) async-start(bf16[64,14,256]{2,1,0:T(8,128)(2,1)} %all_to_all.14), calls=%async_computation.2 | async-start | bytes 1048576 | tf_op jit(solution)/shard_map/all_to_all | solution.py:43
  396.3 0.0 copy-done.2
  396.4 0.1 copy.25
  396.5 0.1 mul.42
  396.7 31.4 %all-to-all-done.1 = bf16[64,14,256]{2,1,0:T(8,128)(2,1)S(1)} async-done(((bf16[64,14,256]{2,1,0:T(8,128)(2,1)}), bf16[64,14,256]{2,1,0:T(8,128)(2,1)S(1)}, u32[]{:S(2)}, u32[]{:S(2)}) %all-to-all-start.1) | async-done | bytes 458784 | tf_op jit(solution)/shard_map/all_to_all | solution.py:43
  428.0 0.1 reshape.102
  428.1 2.1 gather_fusion
  430.3 0.1 reshape.101
  430.4 1.0 multiply_reduce_fusion
  (6 shorter events, 0.1 us)
Async XLA Ops:
  6.5 258.4 %copy-start = (bf16[1,176,2048]{2,1,0:T(8,128)(2,1)S(1)}, bf16[1,176,2048]{2,1,0:T(8,128)(2,1)}, u32[]{:S(2)}) copy-start(bf16[1,176,2048]{2,1,0:T(8,128)(2,1)} %param.11) | copy-start | bytes 2162692
  6.5 372.9 %reduce-scatter.2.cloned.1.call-start = ((), (), s32[]{:S(2)}) async-start(), calls=%async_computation.3 | async-start | bytes 4128768 | tf_op jit(solution)/shard_map/reduce_scatter | solution.py:40
  50.6 209.3 %copy-start.3 = (bf16[1,176,2048]{2,1,0:T(8,128)(2,1)S(1)}, bf16[1,176,2048]{2,1,0:T(8,128)(2,1)}, u32[]{:S(2)}) copy-start(bf16[1,176,2048]{2,1,0:T(8,128)(2,1)} %param.9) | copy-start | bytes 2162692
  258.0 1.9 copy-start.1
  259.9 5.1 %copy-start.4 = (bf16[1,176,2048]{2,1,0:T(8,128)(2,1)S(1)}, bf16[1,176,2048]{2,1,0:T(8,128)(2,1)}, u32[]{:S(2)}) copy-start(bf16[1,176,2048]{2,1,0:T(8,128)(2,1)} %param.10) | copy-start | bytes 2162692
  285.2 111.2 %copy-start.2 = (bf16[128,6]{0,1:T(8,128)(2,1)S(1)}, bf16[128,6]{0,1:T(8,128)(2,1)}, u32[]{:S(2)}) copy-start(bf16[128,6]{0,1:T(8,128)(2,1)} %param.8) | copy-start | bytes 4612
  381.4 46.6 %all-to-all-start.1 = ((bf16[64,14,256]{2,1,0:T(8,128)(2,1)}), bf16[64,14,256]{2,1,0:T(8,128)(2,1)S(1)}, u32[]{:S(2)}, u32[]{:S(2)}) async-start(bf16[64,14,256]{2,1,0:T(8,128)(2,1)} %all_to_all.14), calls=%async_computation.2 | async-start | bytes 1048576 | tf_op jit(solution)/shard_map/all_to_all | solution.py:43
Sparse Core Ops, SparseCore 0:
  285.3 94.0 reduce-scatter.1
where the time goes:
time: 439 us; the launch traced here: 438 us
  blocking collectives  238 us (54%)
  waiting for transfers between devices  126 us (29%)
  local copies, waits for them, and re-layouts  26 us (6%)
  matrix products  16.3 us (4%)
  starting transfers between devices  14.9 us (3%)
  between operations  13.5 us (3%)
    all_to_all x1, blocking collectives, local(): lax.all_to_all(outgoing, 'wide', split_axis=0, concat_axis=0, tiled=True)  207 us
    reduce_scatter x1, waiting for transfers between devices, local(): lax.psum_scatter(partial_value, 'narrow', scatter_dimension=1, tiled=True)  94.2 us
    all_to_all x1, waiting for transfers between devices, local(): lax.all_to_all(summed.astype(jnp.bfloat16), 'wide', split_axis=0, concat_...  31.4 us
    all_gather x1, blocking collectives, local(): whole = lax.all_gather(tokens, 'narrow', axis=1, tiled=True)  31 us
    all_to_all x1, starting transfers between devices, local(): lax.all_to_all(summed.astype(jnp.bfloat16), 'wide', split_axis=0, concat_...  14.9 us
  transfers between devices with their start and end apart: 2, of which 2 were waited for; matrix products, arithmetic and copies ran while one was open for 0% of the time, Pallas kernels for 0%

commit v1 on v0

--- a/solution.py
+++ b/solution.py
@@ -24,7 +24,9 @@
         destination[:, :, None] == jnp.arange(slots_all, dtype=jnp.int32)[None, None, :]
     ).astype(jnp.float32)
     dispatch = jnp.sum(slot_table, axis=1).astype(jnp.bfloat16)
-    whole = lax.all_gather(tokens, "narrow", axis=1, tiled=True)
+    whole = jnp.concatenate(
+        lax.all_to_all(jnp.stack([tokens] * lax.axis_size("narrow")), "narrow", 0, 0), axis=1
+    )
     outgoing = jnp.einsum("ts,td->sd", dispatch, whole, preferred_element_type=jnp.float32).astype(
         jnp.bfloat16
     )

time: 439 us -> 415 us (0.945)
  blocking collectives: 238 us -> 204 us
  starting transfers between devices: 14.9 us -> 22.4 us
    all_gather x1 -> x0, blocking collectives: 31 us -> none  [local(): whole = lax.all_gather(tokens, 'narrow', axis=1, tiled=True)]
    all_to_all x0 -> x1, starting transfers between devices: none -> 7.48 us  [local(): lax.all_to_all(jnp.stack([tokens] * lax.axis_size('narrow')), 'narrow', 0...]
    all_to_all x0 -> x1, waiting for transfers between devices: none -> 5.04 us  [local(): lax.all_to_all(jnp.stack([tokens] * lax.axis_size('narrow')), 'narrow', 0...]
  transfers between devices with their start and end apart: 2 -> 3, of which waited for: 2 -> 3; matrix products, arithmetic and copies ran while one was open for 0% -> 1% of each run, Pallas kernels for 0% -> 0%
where the time goes in v1:
time: 415 us; the launch traced here: 414 us
  blocking collectives  204 us (49%)
  waiting for transfers between devices  128 us (31%)
  local copies, waits for them, and re-layouts  27.8 us (7%)
  starting transfers between devices  22.4 us (5%)
  matrix products  15 us (4%)
  between operations  13.6 us (3%)
    all_to_all x1, blocking collectives, local(): lax.all_to_all(outgoing, 'wide', split_axis=0, concat_axis=0, tiled=True)  204 us
    reduce_scatter x1, waiting for transfers between devices, local(): lax.psum_scatter(partial_value, 'narrow', scatter_dimension=1, tiled=True)  91.1 us
    all_to_all x1, waiting for transfers between devices, local(): lax.all_to_all(summed.astype(jnp.bfloat16), 'wide', split_axis=0, concat_...  31.4 us
    all_to_all x1, starting transfers between devices, local(): lax.all_to_all(summed.astype(jnp.bfloat16), 'wide', split_axis=0, concat_...  14.9 us
  transfers between devices with their start and end apart: 3, of which 3 were waited for; matrix products, arithmetic and copies ran while one was open for 1% of the time, Pallas kernels for 0%

profile of v1, /device:TPU:1, one launch (start us, length us, event | category | flops | bytes accessed | tf_op | source)
XLA Modules:
  0.0 414.1 jit_solution(17556461357383411939)
XLA Ops:
  6.5 0.0 copy-start
  6.5 1.0 copy.33
  7.6 0.9 stack.2
  8.4 7.5 %all-to-all-start = ((bf16[8,128,256]{1,2,0:T(8,128)(2,1)}), bf16[8,128,256]{1,2,0:T(8,128)(2,1)S(1)}, u32[]{:S(2)}, u32[]{:S(2)}) async-start(bf16[8,128,256]{1,2,0:T(8,128)(2,1)} %stack.2), calls=%async_computation | async-start | bytes 1048576 | tf_op jit(solution)/shard_map/all_to_all | solution.py:28
  15.9 0.0 reduce-scatter.2.cloned.1.call-start
  15.9 0.8 copy.28
  16.7 0.1 eq.42
  16.9 0.1 eq.38
  17.0 1.8 reduce-window.6
  18.8 0.3 slice_reduce_fusion
  19.2 0.1 fusion.28
  19.3 0.1 sub.9
  19.5 0.1 copy.32
  19.5 0.4 convert_reduce_fusion
  19.9 5.0 %all-to-all-done = bf16[8,128,256]{1,2,0:T(8,128)(2,1)S(1)} async-done(((bf16[8,128,256]{1,2,0:T(8,128)(2,1)}), bf16[8,128,256]{1,2,0:T(8,128)(2,1)S(1)}, u32[]{:S(2)}, u32[]{:S(2)}) %all-to-all-start) | async-done | bytes 524320 | tf_op jit(solution)/shard_map/all_to_all | solution.py:28
  25.0 3.0 convolution_convert_fusion
  28.0 6.0 %all_to_all.16 = bf16[64,14,2048]{2,1,0:T(8,128)(2,1)} reshape(bf16[896,2048]{1,0:T(8,128)(2,1)} %convolution_convert_fusion) | data formatting | bytes 7340032 | tf_op jit(solution)/shard_map/all_to_all | solution.py:33
  34.0 0.0 copy-start.3
  34.0 204.3 %all_to_all.23 = bf16[64,14,2048]{2,1,0:T(8,128)(2,1)S(1)} all-to-all(bf16[64,14,2048]{2,1,0:T(8,128)(2,1)} %all_to_all.16), channel_id=1, replica_groups=mesh['wide'=64,'narrow'=8] {'wide'}, dimensions={0} | all-to-all | bytes 7340032 | tf_op jit(solution)/shard_map/all_to_all | solution.py:33
  238.2 0.0 copy-start.1
  238.2 1.9 copy-done.1
  240.2 0.0 copy-done.3
  240.2 0.0 copy-start.4
  240.2 4.0 fusion.4
  244.2 0.0 copy-done
  244.2 0.0 copy-done.4
  244.2 8.0 %convert_bitcast_fusion = bf16[64,1,14,2048]{3,0,2,1:T(8,128)(2,1)} fusion(bf16[64,14,2048]{2,1,0:T(8,128)(2,1)} %copy-done.1, f32[64,1,14,176]{3,0,2,1:T(8,128)S(1)} %fusion.4, bf16[1,176,2048]{2,1,0:T(8,128)(2,1)S(1)} %copy-done, bf16[1,176,2048]{2,1,0:T(8,128)(2,1)S(1)} %copy-done.4), kind=kOutput, calls=%fused_computation.1 | convolution fusion | flops 1294626816 | bytes 9412608 | tf_op jit(solution)/shard_map/secf,efd->secd/dot_general | solution.py:38
  252.3 6.0 %copy.36 = bf16[64,1,14,2048]{3,2,0,1:T(8,128)(2,1)} copy(bf16[64,1,14,2048]{3,0,2,1:T(8,128)(2,1)} %convert_bitcast_fusion) | data formatting | bytes 7340032 | tf_op jit(solution)/shard_map/convert_element_type | solution.py:40
  258.3 6.0 %reshape.110 = bf16[896,2048]{1,0:T(8,128)(2,1)} reshape(bf16[64,1,14,2048]{3,2,0,1:T(8,128)(2,1)} %copy.36) | data formatting | bytes 7340032 | tf_op jit(solution)/shard_map/reshape | solution.py:41
  264.2 0.0 copy-start.2
  264.2 0.0 reduce-scatter.2.cloned.1.call-update
  264.2 91.1 %reduce-scatter.2.cloned.1.call-done = bf16[896,256]{1,0:T(8,128)(2,1)} async-done(((bf16[896,2048]{1,0:T(8,128)(2,1)}), bf16[896,256]{1,0:T(8,128)(2,1)}) %reduce-scatter.2.cloned.1.call-update) | async-done | bytes 458768 | tf_op jit(solution)/shard_map/reduce_scatter | solution.py:42
  355.3 1.9 all_to_all.18
  357.3 14.9 %all-to-all-start.2 = ((bf16[64,14,256]{2,1,0:T(8,128)(2,1)}), bf16[64,14,256]{2,1,0:T(8,128)(2,1)S(1)}, u32[]{:S(2)}, u32[]{:S(2)}) async-start(bf16[64,14,256]{2,1,0:T(8,128)(2,1)} %all_to_all.18), calls=%async_computation.3 | async-start | bytes 1048576 | tf_op jit(solution)/shard_map/all_to_all | solution.py:45
  372.2 0.0 copy-done.2
  372.2 0.1 copy.27
  372.3 0.1 mul.42
  372.5 31.4 %all-to-all-done.2 = bf16[64,14,256]{2,1,0:T(8,128)(2,1)S(1)} async-done(((bf16[64,14,256]{2,1,0:T(8,128)(2,1)}), bf16[64,14,256]{2,1,0:T(8,128)(2,1)S(1)}, u32[]{:S(2)}, u32[]{:S(2)}) %all-to-all-start.2) | async-done | bytes 458784 | tf_op jit(solution)/shard_map/all_to_all | solution.py:45
  403.9 0.1 reshape.112
  404.0 2.1 gather_fusion
  406.1 0.1 reshape.111
  406.2 1.0 multiply_reduce_fusion
  (6 shorter events, 0.1 us)
Async XLA Ops:
  6.5 237.7 %copy-start = (bf16[1,176,2048]{2,1,0:T(8,128)(2,1)S(1)}, bf16[1,176,2048]{2,1,0:T(8,128)(2,1)}, u32[]{:S(2)}) copy-start(bf16[1,176,2048]{2,1,0:T(8,128)(2,1)} %param.11) | copy-start | bytes 2162692
  8.4 16.6 %all-to-all-start = ((bf16[8,128,256]{1,2,0:T(8,128)(2,1)}), bf16[8,128,256]{1,2,0:T(8,128)(2,1)S(1)}, u32[]{:S(2)}, u32[]{:S(2)}) async-start(bf16[8,128,256]{1,2,0:T(8,128)(2,1)} %stack.2), calls=%async_computation | async-start | bytes 1048576 | tf_op jit(solution)/shard_map/all_to_all | solution.py:28
  15.9 339.4 %reduce-scatter.2.cloned.1.call-start = ((), (), s32[]{:S(2)}) async-start(), calls=%async_computation.4 | async-start | bytes 4128768 | tf_op jit(solution)/shard_map/reduce_scatter | solution.py:42
  34.0 206.2 %copy-start.3 = (bf16[1,176,2048]{2,1,0:T(8,128)(2,1)S(1)}, bf16[1,176,2048]{2,1,0:T(8,128)(2,1)}, u32[]{:S(2)}) copy-start(bf16[1,176,2048]{2,1,0:T(8,128)(2,1)} %param.9) | copy-start | bytes 2162692
  238.2 1.9 copy-start.1
  240.2 4.0 copy-start.4
  264.2 108.0 %copy-start.2 = (bf16[128,6]{0,1:T(8,128)(2,1)S(1)}, bf16[128,6]{0,1:T(8,128)(2,1)}, u32[]{:S(2)}) copy-start(bf16[128,6]{0,1:T(8,128)(2,1)} %param.8) | copy-start | bytes 4612
  357.3 46.6 %all-to-all-start.2 = ((bf16[64,14,256]{2,1,0:T(8,128)(2,1)}), bf16[64,14,256]{2,1,0:T(8,128)(2,1)S(1)}, u32[]{:S(2)}, u32[]{:S(2)}) async-start(bf16[64,14,256]{2,1,0:T(8,128)(2,1)} %all_to_all.18), calls=%async_computation.3 | async-start | bytes 1048576 | tf_op jit(solution)/shard_map/all_to_all | solution.py:45
Sparse Core Ops, SparseCore 0:
  264.4 90.9 reduce-scatter.1
